TPU v7x, 512 devices: a whole 4x8x8 slice. The times are simulated.
512 devices in a mesh: ctx: 128 (over z, y, core), tp: 4 (over x).
Axes of the slice: x: 4, y: 8, z: 8, core: 2. Of those that a mesh axis runs over, the one named last changes fastest.
Arguments:
- query: bfloat16 [32768, 4096], P('ctx', 'tp'), may hold values from -96 to 96
- key: bfloat16 [32768, 4096], P('ctx', 'tp'), may hold values from -4 to 4
- value: bfloat16 [32768, 4096], P('ctx', 'tp'), may hold values from -6 to 6
- xin: bfloat16 [32768, 4096], P('ctx', 'tp'), may hold values from -1 to 8
- gate_z: bfloat16 [32768, 4096], P('ctx', 'tp'), may hold values from -6 to 6
- w_bc: bfloat16 [4096, 32], P('tp'), may hold values from -1 to 1
- dt_low: bfloat16 [32768, 256], P('ctx'), may hold values from -4 to 9
- dt_proj: bfloat16 [256, 4096], P(None, 'tp'), may hold values from -3 to 3
- dt_bias: float32 [4096], P('tp'), may hold values from -20 to 0
- a_rate: float32 [16, 4096], P(None, 'tp'), may hold values from 1 to 16
- skip: float32 [4096], P('tp'), may hold values from 0.2 to 2
Outputs:
- attended: bfloat16 [32768, 4096], P('ctx', 'tp')
- mixed: bfloat16 [32768, 4096], P('ctx', 'tp')
All inputs are finite; a program needn't handle non-finite values.
Results may differ from a plain program's by a relative error of at most 0.0085.
Values may be sent and summed in bfloat16 or wider, within the bound.
No kernel may reach another device: no remote copies, remote signals or barrier semaphores. Data moves between devices by JAX's collectives and lax.ppermute only.
A program may use at most 128 MiB of HBM per device.

v0:
```python
import jax
import jax.numpy as jnp
from jax import lax
from jax.sharding import PartitionSpec as P

HD = 128
WINDOW = 2048
NS = 16


def passed_along(block, axis, distance):
    devices = range(lax.axis_size(axis))
    route = [(i - distance, i) for i in devices if i - distance in devices]
    return lax.ppermute(block, axis, route)


def entering(shard, axis, combine, identity):
    peers, here = (lax.axis_size(axis), lax.axis_index(axis))
    everything = jax.tree.map(lambda part: lax.all_gather(part, axis), shard)
    start = jax.tree.map(
        lambda part, zero: jnp.broadcast_to(jnp.asarray(zero, part.dtype), part.shape),
        shard,
        identity,
    )

    def step(k, before):
        reached = k < here
        new = combine(before, jax.tree.map(lambda part: part[k], everything))
        return jax.tree.map(lambda a, b: jnp.where(reached, a, b), new, before)

    return lax.fori_loop(0, peers, step, start)


def combine_states(earlier, later):
    return (earlier[0] * later[0], later[0] * earlier[1] + later[1])


def sweep_states(start_state, decay_rates, step_sizes, driven, b_rows, c_rows, with_output):
    tok_rows, channels = step_sizes.shape
    length = 32
    blocks = tok_rows // length
    inputs = (
        step_sizes.reshape(blocks, length, channels),
        driven.reshape(blocks, length, channels),
        b_rows.reshape(blocks, length, b_rows.shape[1]),
        c_rows.reshape(blocks, length, c_rows.shape[1]),
    )

    def advance(carried, block_in):
        sizes_block, drive_block, b_block, c_block = block_in
        outputs = []
        for offset in range(length):
            carried = (
                jnp.exp(-sizes_block[offset][None, :] * decay_rates) * carried
                + drive_block[offset][None, :] * b_block[offset][:, None]
            )
            if with_output:
                outputs.append(jnp.sum(c_block[offset][:, None] * carried, axis=0))
        if with_output:
            return (carried, jnp.stack(outputs))
        return (carried, None)

    last_state, produced = lax.scan(advance, start_state, inputs)
    if with_output:
        return (last_state, produced.reshape(tok_rows, channels))
    return (last_state, None)


def window_attention(query, pieces, place, reach):
    tok_rows = query.shape[0]
    ordered = jnp.concatenate(pieces[::-1], axis=1)
    key_pos = (place - reach) * tok_rows + jnp.arange(ordered.shape[1], dtype=jnp.int32)
    query_pos = place * tok_rows + jnp.arange(tok_rows, dtype=jnp.int32)
    allowed = (
        (key_pos[None, :] <= query_pos[:, None])
        & (key_pos[None, :] > query_pos[:, None] - WINDOW)
        & (key_pos[None, :] >= 0)
    )
    scale = HD ** (-0.5)
    heads_dev = query.shape[1] // HD
    results = []
    for head_num in range(heads_dev):
        column = slice(head_num * HD, (head_num + 1) * HD)
        scores = (
            lax.dot_general(
                query[:, column],
                ordered[0][:, column],
                (((1,), (1,)), ((), ())),
                preferred_element_type=jnp.float32,
            )
            * scale
        )
        masked = jnp.where(allowed, scores, -jnp.inf)
        row_max = jnp.max(masked, axis=1, keepdims=True)
        unscaled = jnp.where(allowed, jnp.exp(scores - row_max), 0.0)
        row_sum = jnp.sum(unscaled, axis=1, keepdims=True)
        probs = (unscaled / row_sum).astype(jnp.bfloat16)
        results.append(
            jnp.dot(probs, ordered[1][:, column], preferred_element_type=jnp.float32).astype(
                jnp.bfloat16
            )
        )
    return jnp.concatenate(results, axis=1)


def shards(query, key, value, xin, gate_z, w_bc, dt_low, dt_proj, dt_bias, a_rate, skip):
    tok_rows = query.shape[0]
    place = lax.axis_index("ctx")
    stacked = jnp.stack([key, value])
    reach = WINDOW // tok_rows
    pieces = [stacked]
    for distance in range(1, reach + 1):
        pieces.append(passed_along(stacked, "ctx", distance))
    partial_bc = jnp.dot(xin, w_bc, preferred_element_type=jnp.float32)
    summed_bc = lax.psum(partial_bc, "tp")
    b_rows = summed_bc[:, :NS]
    c_rows = summed_bc[:, NS:]
    step_sizes = jax.nn.softplus(
        jnp.dot(dt_low, dt_proj, preferred_element_type=jnp.float32) + dt_bias[None, :]
    )
    inputs_float = xin.astype(jnp.float32)
    driven = step_sizes * inputs_float
    zero_state = jnp.zeros((NS, step_sizes.shape[1]), jnp.float32)
    local_end, local_out = sweep_states(
        zero_state, a_rate, step_sizes, driven, b_rows, c_rows, False
    )
    through = jnp.sum(step_sizes, axis=0)
    decay_all = jnp.exp(-a_rate * through[None, :])
    prefix = entering(
        (decay_all, local_end),
        "ctx",
        combine_states,
        (jnp.ones_like(decay_all), jnp.zeros_like(local_end)),
    )
    incoming = prefix[1]
    attended = window_attention(query, pieces, place, reach)
    unused_state, outputs = sweep_states(incoming, a_rate, step_sizes, driven, b_rows, c_rows, True)
    mixed = (
        (outputs + skip[None, :] * inputs_float) * jax.nn.silu(gate_z.astype(jnp.float32))
    ).astype(jnp.bfloat16)
    return (attended, mixed)


def solution(mesh):
    in_specs = (
        P("ctx", "tp"),
        P("ctx", "tp"),
        P("ctx", "tp"),
        P("ctx", "tp"),
        P("ctx", "tp"),
        P("tp", None),
        P("ctx", None),
        P(None, "tp"),
        P("tp"),
        P(None, "tp"),
        P("tp"),
    )
    out_specs = (P("ctx", "tp"), P("ctx", "tp"))
    return jax.shard_map(shards, mesh=mesh, in_specs=in_specs, out_specs=out_specs, check_vma=False)
```

profile of v0, /device:TPU:1, one launch (start us, length us, event | category | flops | bytes accessed | tf_op | source)
XLA Modules:
  0.0 662.3 jit_solution(11239584919717683615)
XLA Ops:
  8.6 14.5 %psum.7 = f32[256,32]{0,1:T(8,128)S(1)} all-reduce(f32[256,32]{0,1:T(8,128)S(1)} %fusion.264), channel_id=1, replica_groups=mesh['ctx'=128,'tp'=4] {'tp'}, use_global_device_ids=true, to_apply=%region_17.18 | all-reduce | flops 8192 | bytes 65536 | tf_op jit(solution)/shard_map/psum | solution.py:115
  23.8 2.5 convert_multiply_fusion.2
  26.3 38.5 %while.38 = (s32[]{:T(128)}, f32[16,1024]{1,0:T(8,128)}, f32[8,32,1024]{2,1,0:T(8,128)S(1)}, f32[16,1024]{1,0:T(8,128)S(1)}, f32[8,32,1024]{2,1,0:T(8,128)S(1)},...) while((s32[]{:T(128)}, f32[16,1024]{1,0:T(8,128)}, ...), condition=%wide.region_19.20_spmd.clone, body=%wide.region_18.19_spmd.clone.sunk | while | flops 2146338 | bytes 990295 | solution.py:63
  33.5 2.3 multiply_add_fusion.42
  38.4 2.3 multiply_add_fusion.42
  43.2 2.3 multiply_add_fusion.42
  48.1 2.3 multiply_add_fusion.42
  52.9 2.3 multiply_add_fusion.42
  67.5 8.1 %collective-permute-start = (bf16[2,256,1024]{2,1,0:T(8,128)(2,1)}, bf16[2,256,1024]{2,1,0:T(8,128)(2,1)}, u32[]{:S(2)}, u32[]{:S(2)}) collective-permute-start(bf16[2,256,1024]{2,1,0:T(8,128)(2,1)} %pad_maximum_fusion), channel_id=1, source_target_pairs={{0,32},{4,36},{8,40},{12,44},{16,48},{20,52},{24,56},{28,60},{32,6... | collective-permute-start | bytes 3145736 | tf_op jit(solution)/shard_map/ppermute | solution.py:14
  75.6 8.2 %collective-permute-start.1 = (bf16[2,256,1024]{2,1,0:T(8,128)(2,1)}, bf16[2,256,1024]{2,1,0:T(8,128)(2,1)}, u32[]{:S(2)}, u32[]{:S(2)}) collective-permute-start(bf16[2,256,1024]{2,1,0:T(8,128)(2,1)} %pad_maximum_fusion), channel_id=1, source_target_pairs={{0,28},{4,32},{8,36},{12,40},{16,44},{20,48},{24,52},{28,56},{32,6... | collective-permute-start | bytes 3145736 | tf_op jit(solution)/shard_map/ppermute | solution.py:14
  83.7 5.2 collective-permute-start.2
  91.2 5.2 collective-permute-start.4
  96.5 9.6 %collective-permute-done = bf16[2,256,1024]{2,1,0:T(8,128)(2,1)} collective-permute-done((bf16[2,256,1024]{2,1,0:T(8,128)(2,1)}, bf16[2,256,1024]{2,1,0:T(8,128)(2,1)}, u32[]{:S(2)}, u32[]{:S(2)}) %collective-permute-start) | collective-permute-done | bytes 1048608 | tf_op jit(solution)/shard_map/ppermute | solution.py:14
  106.0 27.5 %collective-permute-start.5 = (bf16[2,256,1024]{2,1,0:T(8,128)(2,1)}, bf16[2,256,1024]{2,1,0:T(8,128)(2,1)}, u32[]{:S(2)}, u32[]{:S(2)}) collective-permute-start(bf16[2,256,1024]{2,1,0:T(8,128)(2,1)} %pad_maximum_fusion), channel_id=1, source_target_pairs={{0,12},{4,16},{8,20},{12,24},{16,28},{20,32},{24,36},{28,40},{32,4... | collective-permute-start | bytes 3145736 | tf_op jit(solution)/shard_map/ppermute | solution.py:14
  133.7 31.2 %collective-permute-done.1 = bf16[2,256,1024]{2,1,0:T(8,128)(2,1)} collective-permute-done((bf16[2,256,1024]{2,1,0:T(8,128)(2,1)}, bf16[2,256,1024]{2,1,0:T(8,128)(2,1)}, u32[]{:S(2)}, u32[]{:S(2)}) %collective-permute-start.1) | collective-permute-done | bytes 1048608 | tf_op jit(solution)/shard_map/ppermute | solution.py:14
  166.2 66.4 %collective-permute-done.2 = bf16[2,256,1024]{2,1,0:T(8,128)(2,1)} collective-permute-done((bf16[2,256,1024]{2,1,0:T(8,128)(2,1)}, bf16[2,256,1024]{2,1,0:T(8,128)(2,1)}, u32[]{:S(2)}, u32[]{:S(2)}) %collective-permute-start.2) | collective-permute-done | bytes 1048608 | tf_op jit(solution)/shard_map/ppermute | solution.py:14
  232.6 60.1 %collective-permute-start.7 = (bf16[2,256,1024]{2,1,0:T(8,128)(2,1)}, bf16[2,256,1024]{2,1,0:T(8,128)(2,1)S(1)}, u32[]{:S(2)}, u32[]{:S(2)}) collective-permute-start(bf16[2,256,1024]{2,1,0:T(8,128)(2,1)} %pad_maximum_fusion), channel_id=1, source_target_pairs={{0,4},{4,8},{8,12},{12,16},{16,20},{20,24},{24,28},{28,32},{32,36}... | collective-permute-start | bytes 3145736 | tf_op jit(solution)/shard_map/ppermute | solution.py:14
  292.8 2.3 constant_dynamic-update-slice_fusion.8
  297.3 2.3 constant_dynamic-update-slice_fusion.6
  299.7 2.3 constant_dynamic-update-slice_fusion.5
  302.0 9.0 %collective-permute-done.4 = bf16[2,256,1024]{2,1,0:T(8,128)(2,1)} collective-permute-done((bf16[2,256,1024]{2,1,0:T(8,128)(2,1)}, bf16[2,256,1024]{2,1,0:T(8,128)(2,1)}, u32[]{:S(2)}, u32[]{:S(2)}) %collective-permute-start.4) | collective-permute-done | bytes 1048608 | tf_op jit(solution)/shard_map/ppermute | solution.py:14
  311.0 2.3 constant_dynamic-update-slice_fusion.4
  313.3 79.2 %collective-permute-done.5 = bf16[2,256,1024]{2,1,0:T(8,128)(2,1)} collective-permute-done((bf16[2,256,1024]{2,1,0:T(8,128)(2,1)}, bf16[2,256,1024]{2,1,0:T(8,128)(2,1)}, u32[]{:S(2)}, u32[]{:S(2)}) %collective-permute-start.5) | collective-permute-done | bytes 1048608 | tf_op jit(solution)/shard_map/ppermute | solution.py:14
  394.8 25.3 %collective-permute-done.6 = bf16[2,256,1024]{2,1,0:T(8,128)(2,1)S(1)} collective-permute-done((bf16[2,256,1024]{2,1,0:T(8,128)(2,1)}, bf16[2,256,1024]{2,1,0:T(8,128)(2,1)S(1)}, u32[]{:S(2)}, u32[]{:S(2)}) %collective-permute-start.6) | collective-permute-done | bytes 1048608 | tf_op jit(solution)/shard_map/ppermute | solution.py:14
  421.1 14.0 %collective-permute-done.7 = bf16[2,256,1024]{2,1,0:T(8,128)(2,1)S(1)} collective-permute-done((bf16[2,256,1024]{2,1,0:T(8,128)(2,1)}, bf16[2,256,1024]{2,1,0:T(8,128)(2,1)S(1)}, u32[]{:S(2)}, u32[]{:S(2)}) %collective-permute-start.7) | collective-permute-done | bytes 1048608 | tf_op jit(solution)/shard_map/ppermute | solution.py:14
  437.3 7.1 %slice_bitcast_fusion = (bf16[2304,1024]{1,0:T(8,128)(2,1)}, bf16[2304,1024]{1,0:T(8,128)(2,1)S(1)}) fusion(bf16[2,2304,1024]{2,1,0:T(8,128)(2,1)} %constant_dynamic-update-slice_fusion), kind=kLoop, calls=%fused_computation.478 | loop fusion | bytes 18874368 | tf_op jit(solution)/shard_map/squeeze | solution.py:99
  448.3 2.5 fusion.200
  452.2 4.0 fusion.199
  466.4 37.8 %all-gather.5.cloned.1.call-done = f32[2048,1024]{1,0:T(8,128)} async-done(((f32[16,1024]{1,0:T(8,128)}), f32[2048,1024]{1,0:T(8,128)}) %all-gather.5.cloned.1.call-update) | async-done | bytes 8388624 | tf_op jit(solution)/shard_map/all_gather | solution.py:19
  504.2 119.9 %while.39 = (s32[]{:T(128)}, f32[16,1024]{1,0:T(8,128)S(1)}, s32[]{:T(128)}, f32[128,16,1024]{2,1,0:T(8,128)}, f32[128,16,1024]{2,1,0:T(8,128)}, /*index=5*/s32[]{:T(128)}, s32[]{:T(128)}) while((s32[]{:T(128)}, f32[16,1024]{1,0:T(8,128)S(1)}, s32[]{:T(128)}, f32[128,16,1024]{2,1,0:T(8,128)}, f32[128,16,1024]{2,1,0:T(8,128)}, ...), condition=%wide.region_21.22_spmd.clone, body=%wide.region_20.21_spmd.clone.sunk | while | flops 65540 | bytes 262245 | solution.py:31
  624.1 28.7 %while.37 = (s32[]{:T(128)}, f32[16,1024]{1,0:T(8,128)S(1)}, f32[8,32,1024]{2,1,0:T(8,128)}, f32[8,32,1024]{2,1,0:T(8,128)S(1)}, f32[16,1024]{1,0:T(8,128)S(1)},...) while((s32[]{:T(128)}, f32[16,1024]{1,0:T(8,128)S(1)}, ...), condition=%wide.region_55.56_spmd, body=%wide.region_22.55_spmd.sunk | while | flops 4718625 | bytes 3357861 | solution.py:63
  652.8 2.6 fusion.227
  (387 shorter events, 203.2 us)
Async XLA Ops:
  7.2 16.6 %copy-start = (bf16[256,1024]{1,0:T(8,128)(2,1)S(1)}, bf16[256,1024]{1,0:T(8,128)(2,1)}, u32[]{:S(2)}) copy-start(bf16[256,1024]{1,0:T(8,128)(2,1)} %param.24) | copy-start | bytes 1572868
  7.2 459.2 %all-gather.7.cloned.1.call-start = ((), (), s32[]{:S(2)}) async-start(), calls=%async_computation.1 | async-start | bytes 8454144 | tf_op jit(solution)/shard_map/all_gather | solution.py:19
  7.2 19.1 %copy-start.2 = (f32[16,1024]{1,0:T(8,128)S(1)}, f32[16,1024]{1,0:T(8,128)}, u32[]{:S(2)}) copy-start(f32[16,1024]{1,0:T(8,128)} %param.26) | copy-start | bytes 196612
  26.3 40.0 %copy-start.4 = (bf16[256,1024]{1,0:T(8,128)(2,1)S(1)}, bf16[256,1024]{1,0:T(8,128)(2,1)}, u32[]{:S(2)}) copy-start(bf16[256,1024]{1,0:T(8,128)(2,1)} %param.19) | copy-start | bytes 1572868
  26.3 40.0 %copy-start.5 = (bf16[256,1024]{1,0:T(8,128)(2,1)S(1)}, bf16[256,1024]{1,0:T(8,128)(2,1)}, u32[]{:S(2)}) copy-start(bf16[256,1024]{1,0:T(8,128)(2,1)} %param.18) | copy-start | bytes 1572868
  64.9 68.7 %copy-start.7 = (f32[256,16]{0,1:T(8,128)S(1)}, f32[256,16]{0,1:T(8,128)}, u32[]{:S(2)}) copy-start(f32[256,16]{0,1:T(8,128)} %get-tuple-element.564) | copy-start | bytes 49156
  64.9 439.3 %all-gather.5.cloned.1.call-start = ((), (), s32[]{:S(2)}) async-start(), calls=%async_computation | async-start | bytes 8454144 | tf_op jit(solution)/shard_map/all_gather | solution.py:19
  67.5 38.6 %collective-permute-start = (bf16[2,256,1024]{2,1,0:T(8,128)(2,1)}, bf16[2,256,1024]{2,1,0:T(8,128)(2,1)}, u32[]{:S(2)}, u32[]{:S(2)}) collective-permute-start(bf16[2,256,1024]{2,1,0:T(8,128)(2,1)} %pad_maximum_fusion), channel_id=1, source_target_pairs={{0,32},{4,36},{8,40},{12,44},{16,48},{20,52},{24,56},{28,60},{32,6... | collective-permute-start | bytes 3145736 | tf_op jit(solution)/shard_map/ppermute | solution.py:14
  75.6 89.3 %collective-permute-start.1 = (bf16[2,256,1024]{2,1,0:T(8,128)(2,1)}, bf16[2,256,1024]{2,1,0:T(8,128)(2,1)}, u32[]{:S(2)}, u32[]{:S(2)}) collective-permute-start(bf16[2,256,1024]{2,1,0:T(8,128)(2,1)} %pad_maximum_fusion), channel_id=1, source_target_pairs={{0,28},{4,32},{8,36},{12,40},{16,44},{20,48},{24,52},{28,56},{32,6... | collective-permute-start | bytes 3145736 | tf_op jit(solution)/shard_map/ppermute | solution.py:14
  83.7 148.9 %collective-permute-start.2 = (bf16[2,256,1024]{2,1,0:T(8,128)(2,1)}, bf16[2,256,1024]{2,1,0:T(8,128)(2,1)}, u32[]{:S(2)}, u32[]{:S(2)}) collective-permute-start(bf16[2,256,1024]{2,1,0:T(8,128)(2,1)} %pad_maximum_fusion), channel_id=1, source_target_pairs={{0,24},{4,28},{8,32},{12,36},{16,40},{20,44},{24,48},{28,52},{32,5... | collective-permute-start | bytes 3145736 | tf_op jit(solution)/shard_map/ppermute | solution.py:14
  89.0 210.7 %collective-permute-start.3 = (bf16[2,256,1024]{2,1,0:T(8,128)(2,1)}, bf16[2,256,1024]{2,1,0:T(8,128)(2,1)}, u32[]{:S(2)}, u32[]{:S(2)}) collective-permute-start(bf16[2,256,1024]{2,1,0:T(8,128)(2,1)} %pad_maximum_fusion), channel_id=1, source_target_pairs={{0,20},{4,24},{8,28},{12,32},{16,36},{20,40},{24,44},{28,48},{32,5... | collective-permute-start | bytes 3145736 | tf_op jit(solution)/shard_map/ppermute | solution.py:14
  91.2 219.7 %collective-permute-start.4 = (bf16[2,256,1024]{2,1,0:T(8,128)(2,1)}, bf16[2,256,1024]{2,1,0:T(8,128)(2,1)}, u32[]{:S(2)}, u32[]{:S(2)}) collective-permute-start(bf16[2,256,1024]{2,1,0:T(8,128)(2,1)} %pad_maximum_fusion), channel_id=1, source_target_pairs={{0,16},{4,20},{8,24},{12,28},{16,32},{20,36},{24,40},{28,44},{32,4... | collective-permute-start | bytes 3145736 | tf_op jit(solution)/shard_map/ppermute | solution.py:14
  106.0 286.4 %collective-permute-start.5 = (bf16[2,256,1024]{2,1,0:T(8,128)(2,1)}, bf16[2,256,1024]{2,1,0:T(8,128)(2,1)}, u32[]{:S(2)}, u32[]{:S(2)}) collective-permute-start(bf16[2,256,1024]{2,1,0:T(8,128)(2,1)} %pad_maximum_fusion), channel_id=1, source_target_pairs={{0,12},{4,16},{8,20},{12,24},{16,28},{20,32},{24,36},{28,40},{32,4... | collective-permute-start | bytes 3145736 | tf_op jit(solution)/shard_map/ppermute | solution.py:14
  164.8 255.2 %collective-permute-start.6 = (bf16[2,256,1024]{2,1,0:T(8,128)(2,1)}, bf16[2,256,1024]{2,1,0:T(8,128)(2,1)S(1)}, u32[]{:S(2)}, u32[]{:S(2)}) collective-permute-start(bf16[2,256,1024]{2,1,0:T(8,128)(2,1)} %pad_maximum_fusion), channel_id=1, source_target_pairs={{0,8},{4,12},{8,16},{12,20},{16,24},{20,28},{24,32},{28,36},{32,40... | collective-permute-start | bytes 3145736 | tf_op jit(solution)/shard_map/ppermute | solution.py:14
  232.6 202.5 %collective-permute-start.7 = (bf16[2,256,1024]{2,1,0:T(8,128)(2,1)}, bf16[2,256,1024]{2,1,0:T(8,128)(2,1)S(1)}, u32[]{:S(2)}, u32[]{:S(2)}) collective-permute-start(bf16[2,256,1024]{2,1,0:T(8,128)(2,1)} %pad_maximum_fusion), channel_id=1, source_target_pairs={{0,4},{4,8},{8,12},{12,16},{16,20},{20,24},{24,28},{28,32},{32,36}... | collective-permute-start | bytes 3145736 | tf_op jit(solution)/shard_map/ppermute | solution.py:14
  437.3 7.1 %copy-start.6 = (bf16[256,1024]{1,0:T(8,128)(2,1)S(1)}, bf16[256,1024]{1,0:T(8,128)(2,1)}, u32[]{:S(2)}) copy-start(bf16[256,1024]{1,0:T(8,128)(2,1)} %param.17) | copy-start | bytes 1572868
  447.2 3.6 slice-start
  448.3 2.5 slice-start.1
  624.1 28.7 %copy-start.3 = (bf16[256,1024]{1,0:T(8,128)(2,1)S(1)}, bf16[256,1024]{1,0:T(8,128)(2,1)}, u32[]{:S(2)}) copy-start(bf16[256,1024]{1,0:T(8,128)(2,1)} %param.20) | copy-start | bytes 1572868
  624.1 28.7 %copy-start.8 = (f32[1024]{0:T(1024)S(1)}, f32[1024]{0:T(1024)}, u32[]{:S(2)}) copy-start(f32[1024]{0:T(1024)} %param.27) | copy-start | bytes 12292
  652.8 2.6 copy-start.1
Sparse Core Ops, SparseCore 0:
  65.0 344.9 all-gather.6
  413.1 90.9 all-gather.4
where the time goes:
time: 669 us; the launch traced here: 662 us
  waiting for transfers between devices  272 us (41%)
  other arithmetic  169 us (25%)
  starting transfers between devices  118 us (18%)
  local copies, waits for them, and re-layouts  49.5 us (7%)
  matrix products  20.8 us (3%)
  blocking collectives  14.5 us (2%)
  between operations  14.3 us (2%)
    ppermute x8, waiting for transfers between devices, passed_along(): return lax.ppermute(block, axis, route)  235 us
    ppermute x8, starting transfers between devices, passed_along(): return lax.ppermute(block, axis, route)  118 us
    select_n x128, other arithmetic, step(): return jax.tree.map(lambda a, b: jnp.where(reached, a, b), new, before)  117 us
    all_gather x2, waiting for transfers between devices, entering(): everything = jax.tree.map(lambda part: lax.all_gather(part, axis), shard)  37.8 us
    add x8, other arithmetic, advance(): jnp.exp(-sizes_block[offset][None, :] * decay_rates) * carried  18.2 us
    unnamed x32, local copies, waits for them, and re-layouts  17.1 us
    psum x1, blocking collectives, shards(): summed_bc = lax.psum(partial_bc, 'tp')  14.5 us
    reduce_sum x72, other arithmetic, advance(): outputs.append(jnp.sum(c_block[offset][:, None] * carried, axis=0))  14.1 us
  transfers between devices with their start and end apart: 10, of which 8 were waited for; matrix products, arithmetic and copies ran while one was open for 7% of the time, Pallas kernels for 0%

commit v1 on v0

--- a/solution.py
+++ b/solution.py
@@ -112,7 +112,7 @@
     for distance in range(1, reach + 1):
         pieces.append(passed_along(stacked, "ctx", distance))
     partial_bc = jnp.dot(xin, w_bc, preferred_element_type=jnp.float32)
-    summed_bc = lax.psum(partial_bc, "tp")
+    summed_bc = jnp.sum(lax.all_gather(partial_bc, "tp"), axis=0)
     b_rows = summed_bc[:, :NS]
     c_rows = summed_bc[:, NS:]
     step_sizes = jax.nn.softplus(

time: 669 us -> 667 us (level)
    psum x1 -> x0, blocking collectives: 14.5 us -> none  [shards(): summed_bc = lax.psum(partial_bc, 'tp')]
    all_gather x0 -> x1, blocking collectives: none -> 10.4 us  [shards(): summed_bc = jnp.sum(lax.all_gather(partial_bc, 'tp'), axis=0)]
where the time goes in v1:
time: 667 us; the launch traced here: 660 us
  waiting for transfers between devices  275 us (41%)
  other arithmetic  169 us (25%)
  starting transfers between devices  117 us (18%)
  local copies, waits for them, and re-layouts  49.6 us (7%)
  matrix products  20.7 us (3%)
  between operations  14.3 us (2%)
  blocking collectives  10.4 us (2%)
    ppermute x8, waiting for transfers between devices, passed_along(): return lax.ppermute(block, axis, route)  236 us
    select_n x128, other arithmetic, step(): return jax.tree.map(lambda a, b: jnp.where(reached, a, b), new, before)  117 us
    ppermute x8, starting transfers between devices, passed_along(): return lax.ppermute(block, axis, route)  117 us
    all_gather x2, waiting for transfers between devices, entering(): everything = jax.tree.map(lambda part: lax.all_gather(part, axis), shard)  38.6 us
    add x8, other arithmetic, advance(): jnp.exp(-sizes_block[offset][None, :] * decay_rates) * carried  18.2 us
    unnamed x32, local copies, waits for them, and re-layouts  17.1 us
    reduce_sum x72, other arithmetic, advance(): outputs.append(jnp.sum(c_block[offset][:, None] * carried, axis=0))  14.1 us
  transfers between devices with their start and end apart: 10, of which 8 were waited for; matrix products, arithmetic and copies ran while one was open for 7% of the time, Pallas kernels for 0%

profile of v1, /device:TPU:1, one launch (start us, length us, event | category | flops | bytes accessed | tf_op | source)
XLA Modules:
  0.0 659.6 jit_solution(5692601206210254011)
XLA Ops:
  8.6 10.4 %all-gather.1 = f32[1024,32]{0,1:T(8,128)S(1)} all-gather(f32[256,32]{0,1:T(8,128)S(1)} %fusion.264), channel_id=3, replica_groups=mesh['ctx'=128,'tp'=4] {'tp'}, dimensions={0}, use_global_device_ids=true | all-gather | bytes 163840 | tf_op jit(solution)/shard_map/all_gather | solution.py:115
  19.9 2.5 convert_multiply_fusion.2
  22.4 38.5 %while.38 = (s32[]{:T(128)}, f32[16,1024]{1,0:T(8,128)}, f32[8,32,1024]{2,1,0:T(8,128)S(1)}, f32[16,1024]{1,0:T(8,128)S(1)}, f32[8,32,1024]{2,1,0:T(8,128)S(1)},...) while((s32[]{:T(128)}, f32[16,1024]{1,0:T(8,128)}, ...), condition=%wide.region_19.20_spmd.clone, body=%wide.region_18.19_spmd.clone.sunk | while | flops 2146338 | bytes 990295 | solution.py:63
  29.6 2.3 multiply_add_fusion.42
  34.5 2.3 multiply_add_fusion.42
  39.3 2.3 multiply_add_fusion.42
  44.1 2.3 multiply_add_fusion.42
  49.0 2.3 multiply_add_fusion.42
  63.5 8.4 %collective-permute-start = (bf16[2,256,1024]{2,1,0:T(8,128)(2,1)}, bf16[2,256,1024]{2,1,0:T(8,128)(2,1)}, u32[]{:S(2)}, u32[]{:S(2)}) collective-permute-start(bf16[2,256,1024]{2,1,0:T(8,128)(2,1)} %pad_maximum_fusion), channel_id=1, source_target_pairs={{0,32},{4,36},{8,40},{12,44},{16,48},{20,52},{24,56},{28,60},{32,6... | collective-permute-start | bytes 3145736 | tf_op jit(solution)/shard_map/ppermute | solution.py:14
  72.0 7.3 %collective-permute-start.1 = (bf16[2,256,1024]{2,1,0:T(8,128)(2,1)}, bf16[2,256,1024]{2,1,0:T(8,128)(2,1)}, u32[]{:S(2)}, u32[]{:S(2)}) collective-permute-start(bf16[2,256,1024]{2,1,0:T(8,128)(2,1)} %pad_maximum_fusion), channel_id=1, source_target_pairs={{0,28},{4,32},{8,36},{12,40},{16,44},{20,48},{24,52},{28,56},{32,6... | collective-permute-start | bytes 3145736 | tf_op jit(solution)/shard_map/ppermute | solution.py:14
  79.3 5.3 collective-permute-start.2
  86.8 5.2 collective-permute-start.4
  92.0 10.6 %collective-permute-done = bf16[2,256,1024]{2,1,0:T(8,128)(2,1)} collective-permute-done((bf16[2,256,1024]{2,1,0:T(8,128)(2,1)}, bf16[2,256,1024]{2,1,0:T(8,128)(2,1)}, u32[]{:S(2)}, u32[]{:S(2)}) %collective-permute-start) | collective-permute-done | bytes 1048608 | tf_op jit(solution)/shard_map/ppermute | solution.py:14
  102.6 26.8 %collective-permute-start.5 = (bf16[2,256,1024]{2,1,0:T(8,128)(2,1)}, bf16[2,256,1024]{2,1,0:T(8,128)(2,1)}, u32[]{:S(2)}, u32[]{:S(2)}) collective-permute-start(bf16[2,256,1024]{2,1,0:T(8,128)(2,1)} %pad_maximum_fusion), channel_id=1, source_target_pairs={{0,12},{4,16},{8,20},{12,24},{16,28},{20,32},{24,36},{28,40},{32,4... | collective-permute-start | bytes 3145736 | tf_op jit(solution)/shard_map/ppermute | solution.py:14
  129.4 32.7 %collective-permute-done.1 = bf16[2,256,1024]{2,1,0:T(8,128)(2,1)} collective-permute-done((bf16[2,256,1024]{2,1,0:T(8,128)(2,1)}, bf16[2,256,1024]{2,1,0:T(8,128)(2,1)}, u32[]{:S(2)}, u32[]{:S(2)}) %collective-permute-start.1) | collective-permute-done | bytes 1048608 | tf_op jit(solution)/shard_map/ppermute | solution.py:14
  163.5 65.4 %collective-permute-done.2 = bf16[2,256,1024]{2,1,0:T(8,128)(2,1)} collective-permute-done((bf16[2,256,1024]{2,1,0:T(8,128)(2,1)}, bf16[2,256,1024]{2,1,0:T(8,128)(2,1)}, u32[]{:S(2)}, u32[]{:S(2)}) %collective-permute-start.2) | collective-permute-done | bytes 1048608 | tf_op jit(solution)/shard_map/ppermute | solution.py:14
  228.9 60.3 %collective-permute-start.7 = (bf16[2,256,1024]{2,1,0:T(8,128)(2,1)}, bf16[2,256,1024]{2,1,0:T(8,128)(2,1)S(1)}, u32[]{:S(2)}, u32[]{:S(2)}) collective-permute-start(bf16[2,256,1024]{2,1,0:T(8,128)(2,1)} %pad_maximum_fusion), channel_id=1, source_target_pairs={{0,4},{4,8},{8,12},{12,16},{16,20},{20,24},{24,28},{28,32},{32,36}... | collective-permute-start | bytes 3145736 | tf_op jit(solution)/shard_map/ppermute | solution.py:14
  289.2 2.3 constant_dynamic-update-slice_fusion.8
  293.8 2.3 constant_dynamic-update-slice_fusion.6
  296.1 2.3 constant_dynamic-update-slice_fusion.5
  298.4 9.0 %collective-permute-done.4 = bf16[2,256,1024]{2,1,0:T(8,128)(2,1)} collective-permute-done((bf16[2,256,1024]{2,1,0:T(8,128)(2,1)}, bf16[2,256,1024]{2,1,0:T(8,128)(2,1)}, u32[]{:S(2)}, u32[]{:S(2)}) %collective-permute-start.4) | collective-permute-done | bytes 1048608 | tf_op jit(solution)/shard_map/ppermute | solution.py:14
  307.4 2.3 constant_dynamic-update-slice_fusion.4
  309.7 79.5 %collective-permute-done.5 = bf16[2,256,1024]{2,1,0:T(8,128)(2,1)} collective-permute-done((bf16[2,256,1024]{2,1,0:T(8,128)(2,1)}, bf16[2,256,1024]{2,1,0:T(8,128)(2,1)}, u32[]{:S(2)}, u32[]{:S(2)}) %collective-permute-start.5) | collective-permute-done | bytes 1048608 | tf_op jit(solution)/shard_map/ppermute | solution.py:14
  391.5 25.0 %collective-permute-done.6 = bf16[2,256,1024]{2,1,0:T(8,128)(2,1)S(1)} collective-permute-done((bf16[2,256,1024]{2,1,0:T(8,128)(2,1)}, bf16[2,256,1024]{2,1,0:T(8,128)(2,1)S(1)}, u32[]{:S(2)}, u32[]{:S(2)}) %collective-permute-start.6) | collective-permute-done | bytes 1048608 | tf_op jit(solution)/shard_map/ppermute | solution.py:14
  417.6 14.0 %collective-permute-done.7 = bf16[2,256,1024]{2,1,0:T(8,128)(2,1)S(1)} collective-permute-done((bf16[2,256,1024]{2,1,0:T(8,128)(2,1)}, bf16[2,256,1024]{2,1,0:T(8,128)(2,1)S(1)}, u32[]{:S(2)}, u32[]{:S(2)}) %collective-permute-start.7) | collective-permute-done | bytes 1048608 | tf_op jit(solution)/shard_map/ppermute | solution.py:14
  433.7 7.1 %slice_bitcast_fusion = (bf16[2304,1024]{1,0:T(8,128)(2,1)}, bf16[2304,1024]{1,0:T(8,128)(2,1)S(1)}) fusion(bf16[2,2304,1024]{2,1,0:T(8,128)(2,1)} %constant_dynamic-update-slice_fusion), kind=kLoop, calls=%fused_computation.478 | loop fusion | bytes 18874368 | tf_op jit(solution)/shard_map/squeeze | solution.py:99
  444.7 2.5 fusion.200
  448.6 4.0 fusion.199
  462.9 38.6 %all-gather.6.cloned.1.call-done = f32[2048,1024]{1,0:T(8,128)} async-done(((f32[16,1024]{1,0:T(8,128)}), f32[2048,1024]{1,0:T(8,128)}) %all-gather.6.cloned.1.call-update) | async-done | bytes 8388624 | tf_op jit(solution)/shard_map/all_gather | solution.py:19
  501.5 119.9 %while.39 = (s32[]{:T(128)}, f32[16,1024]{1,0:T(8,128)S(1)}, s32[]{:T(128)}, f32[128,16,1024]{2,1,0:T(8,128)}, f32[128,16,1024]{2,1,0:T(8,128)}, /*index=5*/s32[]{:T(128)}, s32[]{:T(128)}) while((s32[]{:T(128)}, f32[16,1024]{1,0:T(8,128)S(1)}, s32[]{:T(128)}, f32[128,16,1024]{2,1,0:T(8,128)}, f32[128,16,1024]{2,1,0:T(8,128)}, ...), condition=%wide.region_21.22_spmd.clone, body=%wide.region_20.21_spmd.clone.sunk | while | flops 65540 | bytes 262245 | solution.py:31
  621.4 28.7 %while.37 = (s32[]{:T(128)}, f32[16,1024]{1,0:T(8,128)S(1)}, f32[8,32,1024]{2,1,0:T(8,128)}, f32[8,32,1024]{2,1,0:T(8,128)S(1)}, f32[16,1024]{1,0:T(8,128)S(1)},...) while((s32[]{:T(128)}, f32[16,1024]{1,0:T(8,128)S(1)}, ...), condition=%wide.region_55.56_spmd, body=%wide.region_22.55_spmd.sunk | while | flops 4718625 | bytes 3357861 | solution.py:63
  650.1 2.6 fusion.227
  (389 shorter events, 203.3 us)
Async XLA Ops:
  7.2 12.7 %copy-start = (bf16[256,1024]{1,0:T(8,128)(2,1)S(1)}, bf16[256,1024]{1,0:T(8,128)(2,1)}, u32[]{:S(2)}) copy-start(bf16[256,1024]{1,0:T(8,128)(2,1)} %param.24) | copy-start | bytes 1572868
  7.2 455.7 %all-gather.8.cloned.1.call-start = ((), (), s32[]{:S(2)}) async-start(), calls=%async_computation.1 | async-start | bytes 8454144 | tf_op jit(solution)/shard_map/all_gather | solution.py:19
  8.6 13.8 %copy-start.2 = (f32[16,1024]{1,0:T(8,128)S(1)}, f32[16,1024]{1,0:T(8,128)}, u32[]{:S(2)}) copy-start(f32[16,1024]{1,0:T(8,128)} %param.26) | copy-start | bytes 196612
  22.4 40.0 %copy-start.4 = (bf16[256,1024]{1,0:T(8,128)(2,1)S(1)}, bf16[256,1024]{1,0:T(8,128)(2,1)}, u32[]{:S(2)}) copy-start(bf16[256,1024]{1,0:T(8,128)(2,1)} %param.19) | copy-start | bytes 1572868
  22.4 40.0 %copy-start.5 = (bf16[256,1024]{1,0:T(8,128)(2,1)S(1)}, bf16[256,1024]{1,0:T(8,128)(2,1)}, u32[]{:S(2)}) copy-start(bf16[256,1024]{1,0:T(8,128)(2,1)} %param.18) | copy-start | bytes 1572868
  61.0 68.4 %copy-start.7 = (f32[256,16]{0,1:T(8,128)S(1)}, f32[256,16]{0,1:T(8,128)}, u32[]{:S(2)}) copy-start(f32[256,16]{0,1:T(8,128)} %get-tuple-element.566) | copy-start | bytes 49156
  61.0 440.5 %all-gather.6.cloned.1.call-start = ((), (), s32[]{:S(2)}) async-start(), calls=%async_computation | async-start | bytes 8454144 | tf_op jit(solution)/shard_map/all_gather | solution.py:19
  63.5 39.0 %collective-permute-start = (bf16[2,256,1024]{2,1,0:T(8,128)(2,1)}, bf16[2,256,1024]{2,1,0:T(8,128)(2,1)}, u32[]{:S(2)}, u32[]{:S(2)}) collective-permute-start(bf16[2,256,1024]{2,1,0:T(8,128)(2,1)} %pad_maximum_fusion), channel_id=1, source_target_pairs={{0,32},{4,36},{8,40},{12,44},{16,48},{20,52},{24,56},{28,60},{32,6... | collective-permute-start | bytes 3145736 | tf_op jit(solution)/shard_map/ppermute | solution.py:14
  72.0 90.1 %collective-permute-start.1 = (bf16[2,256,1024]{2,1,0:T(8,128)(2,1)}, bf16[2,256,1024]{2,1,0:T(8,128)(2,1)}, u32[]{:S(2)}, u32[]{:S(2)}) collective-permute-start(bf16[2,256,1024]{2,1,0:T(8,128)(2,1)} %pad_maximum_fusion), channel_id=1, source_target_pairs={{0,28},{4,32},{8,36},{12,40},{16,44},{20,48},{24,52},{28,56},{32,6... | collective-permute-start | bytes 3145736 | tf_op jit(solution)/shard_map/ppermute | solution.py:14
  79.3 149.7 %collective-permute-start.2 = (bf16[2,256,1024]{2,1,0:T(8,128)(2,1)}, bf16[2,256,1024]{2,1,0:T(8,128)(2,1)}, u32[]{:S(2)}, u32[]{:S(2)}) collective-permute-start(bf16[2,256,1024]{2,1,0:T(8,128)(2,1)} %pad_maximum_fusion), channel_id=1, source_target_pairs={{0,24},{4,28},{8,32},{12,36},{16,40},{20,44},{24,48},{28,52},{32,5... | collective-permute-start | bytes 3145736 | tf_op jit(solution)/shard_map/ppermute | solution.py:14
  84.5 211.6 %collective-permute-start.3 = (bf16[2,256,1024]{2,1,0:T(8,128)(2,1)}, bf16[2,256,1024]{2,1,0:T(8,128)(2,1)}, u32[]{:S(2)}, u32[]{:S(2)}) collective-permute-start(bf16[2,256,1024]{2,1,0:T(8,128)(2,1)} %pad_maximum_fusion), channel_id=1, source_target_pairs={{0,20},{4,24},{8,28},{12,32},{16,36},{20,40},{24,44},{28,48},{32,5... | collective-permute-start | bytes 3145736 | tf_op jit(solution)/shard_map/ppermute | solution.py:14
  86.8 220.6 %collective-permute-start.4 = (bf16[2,256,1024]{2,1,0:T(8,128)(2,1)}, bf16[2,256,1024]{2,1,0:T(8,128)(2,1)}, u32[]{:S(2)}, u32[]{:S(2)}) collective-permute-start(bf16[2,256,1024]{2,1,0:T(8,128)(2,1)} %pad_maximum_fusion), channel_id=1, source_target_pairs={{0,16},{4,20},{8,24},{12,28},{16,32},{20,36},{24,40},{28,44},{32,4... | collective-permute-start | bytes 3145736 | tf_op jit(solution)/shard_map/ppermute | solution.py:14
  102.6 286.7 %collective-permute-start.5 = (bf16[2,256,1024]{2,1,0:T(8,128)(2,1)}, bf16[2,256,1024]{2,1,0:T(8,128)(2,1)}, u32[]{:S(2)}, u32[]{:S(2)}) collective-permute-start(bf16[2,256,1024]{2,1,0:T(8,128)(2,1)} %pad_maximum_fusion), channel_id=1, source_target_pairs={{0,12},{4,16},{8,20},{12,24},{16,28},{20,32},{24,36},{28,40},{32,4... | collective-permute-start | bytes 3145736 | tf_op jit(solution)/shard_map/ppermute | solution.py:14
  162.1 254.4 %collective-permute-start.6 = (bf16[2,256,1024]{2,1,0:T(8,128)(2,1)}, bf16[2,256,1024]{2,1,0:T(8,128)(2,1)S(1)}, u32[]{:S(2)}, u32[]{:S(2)}) collective-permute-start(bf16[2,256,1024]{2,1,0:T(8,128)(2,1)} %pad_maximum_fusion), channel_id=1, source_target_pairs={{0,8},{4,12},{8,16},{12,20},{16,24},{20,28},{24,32},{28,36},{32,40... | collective-permute-start | bytes 3145736 | tf_op jit(solution)/shard_map/ppermute | solution.py:14
  228.9 202.6 %collective-permute-start.7 = (bf16[2,256,1024]{2,1,0:T(8,128)(2,1)}, bf16[2,256,1024]{2,1,0:T(8,128)(2,1)S(1)}, u32[]{:S(2)}, u32[]{:S(2)}) collective-permute-start(bf16[2,256,1024]{2,1,0:T(8,128)(2,1)} %pad_maximum_fusion), channel_id=1, source_target_pairs={{0,4},{4,8},{8,12},{12,16},{16,20},{20,24},{24,28},{28,32},{32,36}... | collective-permute-start | bytes 3145736 | tf_op jit(solution)/shard_map/ppermute | solution.py:14
  433.7 7.1 %copy-start.6 = (bf16[256,1024]{1,0:T(8,128)(2,1)S(1)}, bf16[256,1024]{1,0:T(8,128)(2,1)}, u32[]{:S(2)}) copy-start(bf16[256,1024]{1,0:T(8,128)(2,1)} %param.17) | copy-start | bytes 1572868
  443.7 3.6 slice-start
  444.7 2.5 slice-start.1
  621.4 28.7 %copy-start.3 = (bf16[256,1024]{1,0:T(8,128)(2,1)S(1)}, bf16[256,1024]{1,0:T(8,128)(2,1)}, u32[]{:S(2)}) copy-start(bf16[256,1024]{1,0:T(8,128)(2,1)} %param.20) | copy-start | bytes 1572868
  621.4 28.7 %copy-start.8 = (f32[1024]{0:T(1024)S(1)}, f32[1024]{0:T(1024)}, u32[]{:S(2)}) copy-start(f32[1024]{0:T(1024)} %param.27) | copy-start | bytes 12292
  650.1 2.6 copy-start.1
Sparse Core Ops, SparseCore 0:
  61.1 345.5 all-gather.7
  409.8 91.6 all-gather.5
